TPU v7x, 32 devices: a whole 2x2x4 slice. The times are simulated.
32 devices in a mesh: row: 8 (over z, y), col: 4 (over x, core).
Axes of the slice: x: 2, y: 2, z: 4, core: 2. Of those that a mesh axis runs over, the one named last changes fastest.
Arguments:
- head_deflections: float32 [256, 3, 2, 1024], P('row', None, None, 'col'), may hold values from -6 to 6
- diag_inverse: float32 [2, 1024, 1024], P(None, None, 'col'), may hold values from -1 to 2, as said below
- coupling: float32 [1024, 1024], P(None, 'col'), may hold values from -0.1875 to 0.1875
- panel_factor: float32 [8192, 2, 1024], P('row', None, 'col'), may hold values from -0.125 to 0.125
- trailing: float32 [256, 3, 8192], P('col', None, 'row'), may hold values from -6 to 6
Outputs:
- solved: float32 [256, 3, 2, 1024], P('row', None, None, 'col')
- rest: float32 [256, 3, 8192], P('col', None, 'row')
Inputs may be any that keep to these rules, and one draw needn't show every extreme that they name: Each diag_inverse[p] is lower triangular with a positive diagonal.
All inputs are finite; a program needn't handle non-finite values.
Results may differ from a plain program's by a relative error of at most 0.00007.
Values sent between devices are 32-bit elements; how exact they have to be, the bound alone decides.
No kernel may reach another device: no remote copies, remote signals or barrier semaphores. Data moves between devices by JAX's collectives and lax.ppermute only.
A program may use at most 64 MiB of HBM per device.

v0:
```python
import jax
import jax.numpy as jnp
from jax import lax
from jax.sharding import PartitionSpec as P


def apply_cols(matrix, vectors):
    return lax.dot_general(
        vectors,
        matrix,
        (((2,), (1,)), ((), ())),
        precision=lax.Precision.HIGHEST,
        preferred_element_type=jnp.float32,
    )


def solve_first(block_rhs, diag_inverse):
    return lax.psum_scatter(
        apply_cols(diag_inverse[0], block_rhs), "col", scatter_dimension=2, tiled=True
    )


def solve_second(block_rhs, first_solved, diag_inverse, coupling):
    moved = lax.psum_scatter(
        apply_cols(coupling, first_solved), "col", scatter_dimension=2, tiled=True
    )
    carried = block_rhs - moved
    return lax.psum_scatter(
        apply_cols(diag_inverse[1], carried), "col", scatter_dimension=2, tiled=True
    )


def share_steps(solved_own):
    return lax.all_gather(solved_own, "row", axis=0, tiled=True)


def panel_terms(solved_all, factor):
    return lax.dot_general(
        solved_all,
        factor,
        (((2,), (1,)), ((), ())),
        precision=lax.Precision.HIGHEST,
        preferred_element_type=jnp.float32,
    )


def both_terms(first_all, second_all, panel_factor):
    first_part = panel_terms(first_all, panel_factor[:, 0, :])
    return first_part + panel_terms(second_all, panel_factor[:, 1, :])


def body(head_deflections, diag_inverse, coupling, panel_factor, trailing):
    first_own = solve_first(head_deflections[:, :, 0, :], diag_inverse)
    first_all = share_steps(first_own)
    second_own = solve_second(head_deflections[:, :, 1, :], first_own, diag_inverse, coupling)
    second_all = share_steps(second_own)
    summed = lax.psum_scatter(
        both_terms(first_all, second_all, panel_factor), "col", scatter_dimension=0, tiled=True
    )
    rest = trailing - summed
    solved = jnp.stack([first_own, second_own], axis=2)
    return (solved, rest)


def solution(mesh):
    placed = (
        P("row", None, None, "col"),
        P(None, None, "col"),
        P(None, "col"),
        P("row", None, "col"),
        P("col", None, "row"),
    )
    return jax.shard_map(
        body,
        mesh=mesh,
        in_specs=placed,
        out_specs=(P("row", None, None, "col"), P("col", None, "row")),
        check_vma=False,
    )
```

profile of v0, /device:TPU:0, one launch (start us, length us, event | category | flops | bytes accessed | tf_op | source)
XLA Modules:
  0.0 187.3 jit_solution(2642508243679747117)
XLA Ops:
  7.2 0.0 copy-start
  7.2 0.0 copy-start.1
  7.2 0.0 reduce-scatter.5.cloned.1.call-start
  7.2 1.3 fusion.12
  8.6 3.1 %fusion.5 = f32[32,3,1024]{2,0,1:T(8,128)} fusion(f32[2,1024,256]{2,1,0:T(8,128)} %param.6, f32[32,3,1,256]{3,2,1,0:T(1,128)S(1)} %get-tuple-element.9), kind=kOutput, calls=%fused_computation.8 | convolution fusion | flops 301989888 | bytes 1540096 | tf_op jit(solution)/shard_map/dot_general | solution.py:8
  11.7 0.0 reduce-scatter.5.cloned.1.call-update
  11.7 0.0 reduce-scatter.7.cloned.1.call-start
  11.8 23.7 %reduce-scatter.5.cloned.1.call-done = f32[32,3,256]{2,0,1:T(8,128)} async-done(((f32[32,3,1024]{2,0,1:T(8,128)}), f32[32,3,256]{2,0,1:T(8,128)}) %reduce-scatter.5.cloned.1.call-update) | async-done | bytes 98320 | tf_op jit(solution)/shard_map/reduce_scatter | solution.py:18
  35.4 0.0 copy-done
  35.4 2.8 %fusion.3 = f32[32,3,1024]{2,0,1:T(8,128)} fusion(f32[32,3,256]{2,0,1:T(8,128)} %reduce-scatter.5.cloned.1.call-done, f32[1024,256]{1,0:T(8,128)S(1)} %copy-done), kind=kOutput, calls=%fused_computation.6 | convolution fusion | flops 301989888 | bytes 1540096 | tf_op jit(solution)/shard_map/dot_general | solution.py:8
  38.2 0.0 reduce-scatter.7.cloned.1.call-update
  38.2 0.0 reduce-scatter.9.cloned.1.call-start
  38.3 21.1 %reduce-scatter.7.cloned.1.call-done = f32[32,3,256]{2,0,1:T(8,128)} async-done(((f32[32,3,1024]{2,0,1:T(8,128)}), f32[32,3,256]{2,0,1:T(8,128)}) %reduce-scatter.7.cloned.1.call-update) | async-done | bytes 98320 | tf_op jit(solution)/shard_map/reduce_scatter | solution.py:24
  59.3 0.0 copy-done.1
  59.3 2.8 %fusion.1 = f32[32,3,1024]{2,0,1:T(8,128)} fusion(f32[2,1024,256]{2,1,0:T(8,128)S(1)} %copy-done.1, f32[32,3,256]{2,0,1:T(8,128)} %reduce-scatter.7.cloned.1.call-done, f32[32,3,1,256]{3,2,1,0:T(1,128)S(1)} %get-tuple-element.8), kind=kOutput, calls=%fused_computation.4 | convolution fusion | flops 302014464 | bytes 1638400 | tf_op jit(solution)/shard_map/dot_general | solution.py:8
  62.1 0.0 reduce-scatter.9.cloned.1.call-update
  62.1 0.0 copy-start.2
  62.2 0.0 reduce-scatter.11.cloned.1.call-start
  62.2 4.0 %fusion.11 = (f32[1024,1,256]{2,1,0:T(1,128)S(1)}, f32[1024,1,256]{2,1,0:T(1,128)S(1)}) fusion(f32[1024,2,256]{2,1,0:T(2,128)} %param.8), kind=kLoop, calls=%fused_computation.16 | loop fusion | bytes 4194304 | tf_op jit(solution)/shard_map/slice | solution.py:49
  66.2 0.0 copy-done.2
  66.2 32.2 %all_gather.6 = f32[256,3,256]{2,0,1:T(8,128)S(1)} all-gather(f32[32,3,256]{2,0,1:T(8,128)S(1)} %copy-done.2), channel_id=1, replica_groups=mesh['row'=8,'col'=4] {'row'}, dimensions={0}, use_global_device_ids=true | all-gather | bytes 884736 | tf_op jit(solution)/shard_map/all_gather | solution.py:34
  98.4 4.3 %fusion = f32[256,3,1024]{2,0,1:T(8,128)} fusion(f32[256,3,256]{2,0,1:T(8,128)S(1)} %all_gather.6, f32[1024,1,256]{2,1,0:T(1,128)S(1)} %get-tuple-element.7), kind=kOutput, calls=%fused_computation.3 | convolution fusion | flops 2415919104 | bytes 4980736 | tf_op jit(solution)/shard_map/dot_general | solution.py:38
  102.7 0.0 reduce-scatter.9.cloned.1.call-done
  102.7 31.9 %all_gather.7 = f32[256,3,256]{2,0,1:T(8,128)S(1)} all-gather(f32[32,3,256]{2,0,1:T(8,128)} %reduce-scatter.9.cloned.1.call-done), channel_id=1, replica_groups=mesh['row'=8,'col'=4] {'row'}, dimensions={0}, use_global_device_ids=true | all-gather | bytes 884736 | tf_op jit(solution)/shard_map/all_gather | solution.py:34
  134.6 5.7 %convolution_add_fusion = f32[256,3,1024]{2,0,1:T(8,128)} fusion(f32[256,3,1024]{2,0,1:T(8,128)} %fusion, f32[256,3,256]{2,0,1:T(8,128)S(1)} %all_gather.7, f32[1024,1,256]{2,1,0:T(1,128)S(1)} %get-tuple-element.6), kind=kOutput, calls=%fused_computation | convolution fusion | flops 2416705536 | bytes 8126464 | tf_op jit(solution)/shard_map/dot_general | solution.py:38
  140.3 0.0 copy-start.4
  140.3 0.0 copy-start.3
  140.3 0.0 reduce-scatter.11.cloned.1.call-update
  140.3 0.9 copy-done.4
  141.2 0.8 copy.16
  142.0 36.6 %reduce-scatter.11.cloned.1.call-done = f32[64,3,1024]{2,0,1:T(8,128)} async-done(((f32[256,3,1024]{2,0,1:T(8,128)}), f32[64,3,1024]{2,0,1:T(8,128)}) %reduce-scatter.11.cloned.1.call-update) | async-done | bytes 786448 | tf_op jit(solution)/shard_map/reduce_scatter | solution.py:57
  178.6 0.0 copy-done.3
  178.6 2.1 %sub.7 = f32[64,3,1024]{2,0,1:T(8,128)} subtract(f32[64,3,1024]{2,0,1:T(8,128)S(1)} %copy-done.3, f32[64,3,1024]{2,0,1:T(8,128)} %reduce-scatter.11.cloned.1.call-done) | non-fusion elementwise | flops 196608 | bytes 2359296 | tf_op jit(solution)/shard_map/sub | solution.py:60
  (1 shorter events, 0.0 us)
Async XLA Ops:
  7.2 28.3 %copy-start = (f32[1024,256]{1,0:T(8,128)S(1)}, f32[1024,256]{1,0:T(8,128)}, u32[]{:S(2)}) copy-start(f32[1024,256]{1,0:T(8,128)} %param.7) | copy-start | bytes 3145732
  7.2 52.2 %copy-start.1 = (f32[2,1024,256]{2,1,0:T(8,128)S(1)}, f32[2,1024,256]{2,1,0:T(8,128)}, u32[]{:S(2)}) copy-start(f32[2,1024,256]{2,1,0:T(8,128)} %param.6) | copy-start | bytes 6291460
  7.2 28.2 %reduce-scatter.5.cloned.1.call-start = ((), (), s32[]{:S(2)}) async-start(), calls=%async_computation.4 | async-start | bytes 491520 | tf_op jit(solution)/shard_map/reduce_scatter | solution.py:18
  11.7 47.6 %reduce-scatter.7.cloned.1.call-start = ((), (), s32[]{:S(2)}) async-start(), calls=%async_computation.5 | async-start | bytes 491520 | tf_op jit(solution)/shard_map/reduce_scatter | solution.py:24
  38.2 64.5 %reduce-scatter.9.cloned.1.call-start = ((), (), s32[]{:S(2)}) async-start(), calls=%async_computation.6 | async-start | bytes 491520 | tf_op jit(solution)/shard_map/reduce_scatter | solution.py:28
  62.1 4.1 %copy-start.2 = (f32[32,3,256]{2,0,1:T(8,128)S(1)}, f32[32,3,256]{2,0,1:T(8,128)}, u32[]{:S(2)}) copy-start(f32[32,3,256]{2,0,1:T(8,128)} %reduce-scatter.5.cloned.1.call-done) | copy-start | bytes 294916
  62.2 116.5 %reduce-scatter.11.cloned.1.call-start = ((), (), s32[]{:S(2)}) async-start(), calls=%async_computation.7 | async-start | bytes 3932160 | tf_op jit(solution)/shard_map/reduce_scatter | solution.py:57
  140.3 0.9 copy-start.4
  140.3 38.4 %copy-start.3 = (f32[64,3,1024]{2,0,1:T(8,128)S(1)}, f32[64,3,1024]{2,0,1:T(8,128)}, u32[]{:S(2)}) copy-start(f32[64,3,1024]{2,0,1:T(8,128)} %param.9) | copy-start | bytes 2359300
Sparse Core Ops, SparseCore 0:
  11.8 23.5 reduce-scatter.4
  38.5 20.8 reduce-scatter.6
  62.4 20.8 reduce-scatter.8
  140.4 38.1 reduce-scatter.10
where the time goes:
time: 188 us; the launch traced here: 187 us
  waiting for transfers between devices  81.4 us (43%)
  blocking collectives  64 us (34%)
  matrix products  18.7 us (10%)
  between operations  13.8 us (7%)
  local copies, waits for them, and re-layouts  7.09 us (4%)
  other arithmetic  2.12 us (1%)
    all_gather x2, blocking collectives, share_steps(): return lax.all_gather(solved_own, 'row', axis=0, tiled=True)  64 us
    reduce_scatter x1, waiting for transfers between devices, body(): lax.psum_scatter(both_terms(first_all, second_all, panel_factor), 'col',...  36.6 us
    reduce_scatter x1, waiting for transfers between devices, solve_first(): lax.psum_scatter(apply_cols(diag_inverse[0], block_rhs), 'col', scatter_d...  23.7 us
    reduce_scatter x1, waiting for transfers between devices, solve_second(): lax.psum_scatter(apply_cols(coupling, first_solved), 'col', scatter_dimen...  21.1 us
    dot_general x2, matrix products, panel_terms(): lax.dot_general(solved_all, factor, (((2,), (1,)), ((), ())), precision=l...  10 us
    dot_general x3, matrix products, apply_cols(): lax.dot_general(vectors, matrix, (((2,), (1,)), ((), ())), precision=lax....  8.65 us
    slice x1, local copies, waits for them, and re-layouts, both_terms(): return first_part + panel_terms(second_all, panel_factor[:, 1, :])  4.02 us
  transfers between devices with their start and end apart: 4, of which 3 were waited for; matrix products, arithmetic and copies ran while one was open for 5% of the time, Pallas kernels for 0%

commit v1 on v0

--- a/solution.py
+++ b/solution.py
@@ -31,7 +31,22 @@
 
 
 def share_steps(solved_own):
-    return lax.all_gather(solved_own, "row", axis=0, tiled=True)
+
+    def register_view(inp, where_dim):
+        k_now = lax.psum(1, "row")
+        clean = lax.axis_index("row")
+        local_now, outer, inter = (k_now, clean, inp.shape[where_dim])
+        carry, last = (inp, 1)
+        while last < local_now:
+            f_next = lax.ppermute(
+                carry, "row", [(nth, (nth - last) % local_now) for nth in range(local_now)]
+            )
+            carry = jnp.concatenate([carry, f_next], axis=where_dim)
+            last = 2 * last
+        u1 = jnp.roll(carry, outer * inter, axis=where_dim)
+        return u1
+
+    return register_view(solved_own, where_dim=0)
 
 
 def panel_terms(solved_all, factor):

time: 188 us -> 190 us (1.011)
  blocking collectives: 64 us -> 0 us
  waiting for transfers between devices: 81.4 us -> 136 us
  starting transfers between devices: 0.16 us -> 8.75 us
  other arithmetic: 2.12 us -> 5.6 us
    all_gather x2 -> x0, blocking collectives: 64 us -> none  [share_steps(): return lax.all_gather(solved_own, 'row', axis=0, tiled=True)]
    ppermute x0 -> x6, waiting for transfers between devices: none -> 30.3 us  [register_view(): lax.ppermute(carry, 'row', [(nth, (nth - last) % local_now) for nth in ra...]
    reduce_scatter x1, waiting for transfers between devices: 0.01 us -> 21.1 us  [solve_second(): lax.psum_scatter(apply_cols(diag_inverse[1], carried), 'col', scatter_dim...]
    ppermute x0 -> x6, starting transfers between devices: none -> 8.58 us  [register_view(): lax.ppermute(carry, 'row', [(nth, (nth - last) % local_now) for nth in ra...]
    concatenate x0 -> x4, other arithmetic: none -> 3.48 us  [register_view(): carry = jnp.concatenate([carry, f_next], axis=where_dim)]
    reduce_scatter x1, waiting for transfers between devices: 36.6 us -> 40 us  [body(): lax.psum_scatter(both_terms(first_all, second_all, panel_factor), 'col',...]
  transfers between devices with their start and end apart: 4 -> 10, of which waited for: 3 -> 9; matrix products, arithmetic and copies ran while one was open for 5% -> 7% of each run, Pallas kernels for 0% -> 0%
where the time goes in v1:
time: 190 us; the launch traced here: 189 us
  waiting for transfers between devices  136 us (72%)
  matrix products  18.8 us (10%)
  between operations  13.8 us (7%)
  starting transfers between devices  8.75 us (5%)
  local copies, waits for them, and re-layouts  6.16 us (3%)
  other arithmetic  5.6 us (3%)
    reduce_scatter x1, waiting for transfers between devices, body(): lax.psum_scatter(both_terms(first_all, second_all, panel_factor), 'col',...  40 us
    ppermute x6, waiting for transfers between devices, register_view(): lax.ppermute(carry, 'row', [(nth, (nth - last) % local_now) for nth in ra...  30.3 us
    reduce_scatter x1, waiting for transfers between devices, solve_first(): lax.psum_scatter(apply_cols(diag_inverse[0], block_rhs), 'col', scatter_d...  23.7 us
    reduce_scatter x1, waiting for transfers between devices, solve_second(): lax.psum_scatter(apply_cols(diag_inverse[1], carried), 'col', scatter_dim...  21.1 us
    reduce_scatter x1, waiting for transfers between devices, solve_second(): lax.psum_scatter(apply_cols(coupling, first_solved), 'col', scatter_dimen...  21.1 us
    dot_general x2, matrix products, panel_terms(): lax.dot_general(solved_all, factor, (((2,), (1,)), ((), ())), precision=l...  10.1 us
    dot_general x3, matrix products, apply_cols(): lax.dot_general(vectors, matrix, (((2,), (1,)), ((), ())), precision=lax....  8.79 us
    ppermute x6, starting transfers between devices, register_view(): lax.ppermute(carry, 'row', [(nth, (nth - last) % local_now) for nth in ra...  8.58 us
  transfers between devices with their start and end apart: 10, of which 9 were waited for; matrix products, arithmetic and copies ran while one was open for 7% of the time, Pallas kernels for 0%

profile of v1, /device:TPU:0, one launch (start us, length us, event | category | flops | bytes accessed | tf_op | source)
XLA Modules:
  0.0 189.4 jit_solution(3946796657077684964)
XLA Ops:
  7.2 0.0 copy-start
  7.2 0.0 reduce-scatter.5.cloned.1.call-start
  7.2 1.3 fusion.34
  8.5 0.0 copy-start.2
  8.5 3.2 %fusion.5 = f32[32,3,1024]{2,0,1:T(8,128)} fusion(f32[2,1024,256]{2,1,0:T(8,128)} %param.8, f32[32,3,1,256]{3,2,1,0:T(1,128)S(1)} %get-tuple-element.10), kind=kOutput, calls=%fused_computation.24 | convolution fusion | flops 301989888 | bytes 1540096 | tf_op jit(solution)/shard_map/dot_general | solution.py:8
  11.8 0.0 reduce-scatter.5.cloned.1.call-update
  11.8 0.0 reduce-scatter.7.cloned.1.call-start
  11.8 23.7 %reduce-scatter.5.cloned.1.call-done = f32[32,3,256]{2,0,1:T(8,128)} async-done(((f32[32,3,1024]{2,0,1:T(8,128)}), f32[32,3,256]{2,0,1:T(8,128)}) %reduce-scatter.5.cloned.1.call-update) | async-done | bytes 98320 | tf_op jit(solution)/shard_map/reduce_scatter | solution.py:18
  35.5 0.0 copy-done
  35.5 2.8 %fusion.3 = f32[32,3,1024]{2,0,1:T(8,128)} fusion(f32[32,3,256]{2,0,1:T(8,128)} %reduce-scatter.5.cloned.1.call-done, f32[1024,256]{1,0:T(8,128)S(1)} %copy-done), kind=kOutput, calls=%fused_computation.22 | convolution fusion | flops 301989888 | bytes 1540096 | tf_op jit(solution)/shard_map/dot_general | solution.py:8
  38.3 0.0 copy-start.1
  38.3 0.0 reduce-scatter.7.cloned.1.call-update
  38.3 0.0 reduce-scatter.9.cloned.1.call-start
  38.3 21.1 %reduce-scatter.7.cloned.1.call-done = f32[32,3,256]{2,0,1:T(8,128)} async-done(((f32[32,3,1024]{2,0,1:T(8,128)}), f32[32,3,256]{2,0,1:T(8,128)}) %reduce-scatter.7.cloned.1.call-update) | async-done | bytes 98320 | tf_op jit(solution)/shard_map/reduce_scatter | solution.py:24
  59.4 0.0 copy-done.2
  59.4 2.8 %fusion.1 = f32[32,3,1024]{2,0,1:T(8,128)} fusion(f32[2,1024,256]{2,1,0:T(8,128)S(1)} %copy-done.2, f32[32,3,256]{2,0,1:T(8,128)} %reduce-scatter.7.cloned.1.call-done, f32[32,3,1,256]{3,2,1,0:T(1,128)S(1)} %get-tuple-element.9), kind=kOutput, calls=%fused_computation.20 | convolution fusion | flops 302014464 | bytes 1638400 | tf_op jit(solution)/shard_map/dot_general | solution.py:8
  62.2 0.0 reduce-scatter.9.cloned.1.call-update
  62.2 0.0 reduce-scatter.11.cloned.1.call-start
  62.3 21.1 %reduce-scatter.9.cloned.1.call-done = f32[32,3,256]{2,0,1:T(8,128)} async-done(((f32[32,3,1024]{2,0,1:T(8,128)}), f32[32,3,256]{2,0,1:T(8,128)}) %reduce-scatter.9.cloned.1.call-update) | async-done | bytes 98320 | tf_op jit(solution)/shard_map/reduce_scatter | solution.py:28
  83.3 4.2 %collective-permute-start.3 = (f32[32,3,256]{2,0,1:T(8,128)}, f32[32,3,256]{2,0,1:T(8,128)S(1)}, u32[]{:S(2)}, u32[]{:S(2)}) collective-permute-start(f32[32,3,256]{2,0,1:T(8,128)} %reduce-scatter.9.cloned.1.call-done), channel_id=1, source_target_pairs={{0,28},{4,0},{8,4},{12,8},{16,12},{20,16},{24,20},{28,24},{1,29},{... | collective-permute-start | bytes 294920 | tf_op jit(solution)/shard_map/ppermute | solution.py:41
  87.6 0.0 copy-done.1
  87.6 0.6 collective-permute-start
  88.1 2.7 %collective-permute-done.3 = f32[32,3,256]{2,0,1:T(8,128)S(1)} collective-permute-done((f32[32,3,256]{2,0,1:T(8,128)}, f32[32,3,256]{2,0,1:T(8,128)S(1)}, u32[]{:S(2)}, u32[]{:S(2)}) %collective-permute-start.3) | collective-permute-done | bytes 98336 | tf_op jit(solution)/shard_map/ppermute | solution.py:41
  90.8 0.9 pad_maximum_fusion.4
  91.7 1.5 collective-permute-start.4
  93.3 0.0 collective-permute-done
  93.3 0.8 collective-permute-start.1
  94.0 4.8 %collective-permute-done.4 = f32[64,3,256]{2,0,1:T(8,128)S(1)} collective-permute-done((f32[64,3,256]{2,0,1:T(8,128)S(1)}, f32[64,3,256]{2,0,1:T(8,128)S(1)}, u32[]{:S(2)}, u32[]{:S(2)}) %collective-permute-start.4) | collective-permute-done | bytes 196640 | tf_op jit(solution)/shard_map/ppermute | solution.py:41
  98.8 0.0 copy-start.7
  98.8 1.7 pad_maximum_fusion.1
  100.5 0.9 collective-permute-start.5
  101.4 1.4 collective-permute-done.1
  102.8 0.8 pad_maximum_fusion
  103.6 0.0 copy-done.7
  103.6 0.0 copy-done.5
  103.6 0.7 collective-permute-start.2
  104.3 4.0 %fusion.33 = (f32[1024,1,256]{2,1,0:T(1,128)S(1)}, f32[1024,1,256]{2,1,0:T(1,128)S(1)}) fusion(f32[1024,2,256]{2,1,0:T(2,128)} %param.10), kind=kLoop, calls=%fused_computation.54 | loop fusion | bytes 4194304 | tf_op jit(solution)/shard_map/slice | solution.py:63
  108.4 18.3 %collective-permute-done.5 = f32[128,3,256]{2,0,1:T(8,128)} collective-permute-done((f32[128,3,256]{2,0,1:T(8,128)}, f32[128,3,256]{2,0,1:T(8,128)}, u32[]{:S(2)}, u32[]{:S(2)}) %collective-permute-start.5) | collective-permute-done | bytes 393248 | tf_op jit(solution)/shard_map/ppermute | solution.py:41
  126.7 0.0 copy-done.3
  126.7 4.3 %fusion = f32[256,3,1024]{2,0,1:T(8,128)S(1)} fusion(f32[1024,1,256]{2,1,0:T(1,128)S(1)} %get-tuple-element.8, s32[]{:T(128)S(6)} %select_n.13, f32[32,3,256]{2,0,1:T(8,128)S(1)} %copy-done.3, f32[32,3,256]{2,0,1:T(8,128)S(1)} %collective-permute-done.3, f32[64,3,256]{2,0,1:T(8,128)} %copy-done.7, f32[128,3,256]{2,0,1:T(8,128)} %collective-permute-done.5), kind=kOutput, calls=%fused_computation.18 | convolution fusion | flops 2417295360 | bytes 4980740 | tf_op jit(solution)/shard_map/dot_general | solution.py:53
  131.0 3.1 %collective-permute-done.2 = f32[128,3,256]{2,0,1:T(8,128)} collective-permute-done((f32[128,3,256]{2,0,1:T(8,128)}, f32[128,3,256]{2,0,1:T(8,128)}, u32[]{:S(2)}, u32[]{:S(2)}) %collective-permute-start.2) | collective-permute-done | bytes 393248 | tf_op jit(solution)/shard_map/ppermute | solution.py:41
  134.1 0.0 copy-done.6
  134.1 5.8 %convolution_add_fusion = f32[256,3,1024]{2,0,1:T(8,128)} fusion(f32[256,3,1024]{2,0,1:T(8,128)S(1)} %fusion, f32[1024,1,256]{2,1,0:T(1,128)S(1)} %get-tuple-element.7, s32[]{:T(128)S(6)} %select_n.13, f32[32,3,256]{2,0,1:T(8,128)S(1)} %copy-done.1, f32[32,3,256]{2,0,1:T(8,128)S(1)} %collective-permute-done, f32[64,3,256]{2,0,1:T(8,128)S(1)} %copy-done.6, ...), kind=kOutput, calls=%fused_computation | convolution fusion | flops 2418081792 | bytes 8126468 | tf_op jit(solution)/shard_map/dot_general | solution.py:53
  139.9 0.0 reduce-scatter.11.cloned.1.call-update
  139.9 0.8 copy.16
  140.8 40.0 %reduce-scatter.11.cloned.1.call-done = f32[64,3,1024]{2,0,1:T(8,128)} async-done(((f32[256,3,1024]{2,0,1:T(8,128)}), f32[64,3,1024]{2,0,1:T(8,128)}) %reduce-scatter.11.cloned.1.call-update) | async-done | bytes 786448 | tf_op jit(solution)/shard_map/reduce_scatter | solution.py:72
  180.7 0.0 copy-done.4
  180.7 2.1 %sub.10 = f32[64,3,1024]{2,0,1:T(8,128)} subtract(f32[64,3,1024]{2,0,1:T(8,128)S(1)} %copy-done.4, f32[64,3,1024]{2,0,1:T(8,128)} %reduce-scatter.11.cloned.1.call-done) | non-fusion elementwise | flops 196608 | bytes 2359296 | tf_op jit(solution)/shard_map/sub | solution.py:75
  (6 shorter events, 0.0 us)
Async XLA Ops:
  7.2 28.3 %copy-start = (f32[1024,256]{1,0:T(8,128)S(1)}, f32[1024,256]{1,0:T(8,128)}, u32[]{:S(2)}) copy-start(f32[1024,256]{1,0:T(8,128)} %param.9) | copy-start | bytes 3145732
  7.2 28.3 %reduce-scatter.5.cloned.1.call-start = ((), (), s32[]{:S(2)}) async-start(), calls=%async_computation.4 | async-start | bytes 491520 | tf_op jit(solution)/shard_map/reduce_scatter | solution.py:18
  8.5 50.9 %copy-start.2 = (f32[2,1024,256]{2,1,0:T(8,128)S(1)}, f32[2,1024,256]{2,1,0:T(8,128)}, u32[]{:S(2)}) copy-start(f32[2,1024,256]{2,1,0:T(8,128)} %param.8) | copy-start | bytes 6291460
  11.8 47.6 %reduce-scatter.7.cloned.1.call-start = ((), (), s32[]{:S(2)}) async-start(), calls=%async_computation.5 | async-start | bytes 491520 | tf_op jit(solution)/shard_map/reduce_scatter | solution.py:24
  38.3 49.3 %copy-start.1 = (f32[32,3,256]{2,0,1:T(8,128)S(1)}, f32[32,3,256]{2,0,1:T(8,128)}, u32[]{:S(2)}) copy-start(f32[32,3,256]{2,0,1:T(8,128)} %reduce-scatter.5.cloned.1.call-done) | copy-start | bytes 294916
  38.3 45.0 %reduce-scatter.9.cloned.1.call-start = ((), (), s32[]{:S(2)}) async-start(), calls=%async_computation.6 | async-start | bytes 491520 | tf_op jit(solution)/shard_map/reduce_scatter | solution.py:28
  62.2 118.5 %reduce-scatter.11.cloned.1.call-start = ((), (), s32[]{:S(2)}) async-start(), calls=%async_computation.7 | async-start | bytes 3932160 | tf_op jit(solution)/shard_map/reduce_scatter | solution.py:72
  83.3 7.5 %collective-permute-start.3 = (f32[32,3,256]{2,0,1:T(8,128)}, f32[32,3,256]{2,0,1:T(8,128)S(1)}, u32[]{:S(2)}, u32[]{:S(2)}) collective-permute-start(f32[32,3,256]{2,0,1:T(8,128)} %reduce-scatter.9.cloned.1.call-done), channel_id=1, source_target_pairs={{0,28},{4,0},{8,4},{12,8},{16,12},{20,16},{24,20},{28,24},{1,29},{... | collective-permute-start | bytes 294920 | tf_op jit(solution)/shard_map/ppermute | solution.py:41
  87.6 5.7 %collective-permute-start = (f32[32,3,256]{2,0,1:T(8,128)S(1)}, f32[32,3,256]{2,0,1:T(8,128)S(1)}, u32[]{:S(2)}, u32[]{:S(2)}) collective-permute-start(f32[32,3,256]{2,0,1:T(8,128)S(1)} %copy-done.1), channel_id=1, source_target_pairs={{0,28},{4,0},{8,4},{12,8},{16,12},{20,16},{24,20},{28,24},{1,29},{... | collective-permute-start | bytes 294920 | tf_op jit(solution)/shard_map/ppermute | solution.py:41
  91.7 7.1 %collective-permute-start.4 = (f32[64,3,256]{2,0,1:T(8,128)S(1)}, f32[64,3,256]{2,0,1:T(8,128)S(1)}, u32[]{:S(2)}, u32[]{:S(2)}) collective-permute-start(f32[64,3,256]{2,0,1:T(8,128)S(1)} %pad_maximum_fusion.4), channel_id=1, source_target_pairs={{0,24},{4,28},{8,0},{12,4},{16,8},{20,12},{24,16},{28,20},{1,25},{... | collective-permute-start | bytes 589832 | tf_op jit(solution)/shard_map/ppermute | solution.py:41
  93.3 9.5 %collective-permute-start.1 = (f32[64,3,256]{2,0,1:T(8,128)S(1)}, f32[64,3,256]{2,0,1:T(8,128)S(1)}, u32[]{:S(2)}, u32[]{:S(2)}) collective-permute-start(f32[64,3,256]{2,0,1:T(8,128)S(1)} %pad_maximum_fusion.3), channel_id=1, source_target_pairs={{0,24},{4,28},{8,0},{12,4},{16,8},{20,12},{24,16},{28,20},{1,25},{... | collective-permute-start | bytes 589832 | tf_op jit(solution)/shard_map/ppermute | solution.py:41
  98.8 4.8 %copy-start.7 = (f32[64,3,256]{2,0,1:T(8,128)}, f32[64,3,256]{2,0,1:T(8,128)S(1)}, u32[]{:S(2)}) copy-start(f32[64,3,256]{2,0,1:T(8,128)S(1)} %collective-permute-done.4) | copy-start | bytes 589828
  100.5 26.1 %collective-permute-start.5 = (f32[128,3,256]{2,0,1:T(8,128)}, f32[128,3,256]{2,0,1:T(8,128)}, u32[]{:S(2)}, u32[]{:S(2)}) collective-permute-start(f32[128,3,256]{2,0,1:T(8,128)} %pad_maximum_fusion.1), channel_id=1, source_target_pairs={{0,16},{4,20},{8,24},{12,28},{16,0},{20,4},{24,8},{28,12},{1,17},{... | collective-permute-start | bytes 1179656 | tf_op jit(solution)/shard_map/ppermute | solution.py:41
  102.8 0.8 copy-start.5
  103.6 23.1 %copy-start.3 = (f32[32,3,256]{2,0,1:T(8,128)S(1)}, f32[32,3,256]{2,0,1:T(8,128)}, u32[]{:S(2)}) copy-start(f32[32,3,256]{2,0,1:T(8,128)} %reduce-scatter.9.cloned.1.call-done) | copy-start | bytes 294916
  103.6 30.4 %collective-permute-start.2 = (f32[128,3,256]{2,0,1:T(8,128)}, f32[128,3,256]{2,0,1:T(8,128)}, u32[]{:S(2)}, u32[]{:S(2)}) collective-permute-start(f32[128,3,256]{2,0,1:T(8,128)} %pad_maximum_fusion), channel_id=1, source_target_pairs={{0,16},{4,20},{8,24},{12,28},{16,0},{20,4},{24,8},{28,12},{1,17},{... | collective-permute-start | bytes 1179656 | tf_op jit(solution)/shard_map/ppermute | solution.py:41
  126.7 7.4 %copy-start.6 = (f32[64,3,256]{2,0,1:T(8,128)S(1)}, f32[64,3,256]{2,0,1:T(8,128)}, u32[]{:S(2)}) copy-start(f32[64,3,256]{2,0,1:T(8,128)} %copy-done.5) | copy-start | bytes 589828
  139.9 40.8 %copy-start.4 = (f32[64,3,1024]{2,0,1:T(8,128)S(1)}, f32[64,3,1024]{2,0,1:T(8,128)}, u32[]{:S(2)}) copy-start(f32[64,3,1024]{2,0,1:T(8,128)} %param.11) | copy-start | bytes 2359300
Sparse Core Ops, SparseCore 0:
  11.9 23.5 reduce-scatter.4
  38.6 20.8 reduce-scatter.6
  62.5 20.8 reduce-scatter.8
  140.0 40.6 reduce-scatter.10
